TPU v7x, 256 devices: a whole 4x4x8 slice. The times are simulated.
256 devices in a mesh: grp: 8 (over z_hi, core), mem: 32 (over y, x, z_lo).
Axes of the slice: x: 4, y: 4, z: 8 (z_hi: 4, z_lo: 2; z = z_hi * 2 + z_lo), core: 2. Of those that a mesh axis runs over, the one named last changes fastest.
Arguments:
- spectra: bfloat16 [3072, 64, 384], P(('grp', 'mem')), may hold values from -45 to 45
Outputs:
- correlations: bfloat16 [7, 8, 384, 32, 12, 128], P(None, 'grp', None, 'mem')
All inputs are finite; a program needn't handle non-finite values.
Results may differ from a plain program's by a relative error of at most 0.0067.
Values may be sent and summed in bfloat16 or wider, within the bound.
No kernel may reach another device: no remote copies, remote signals or barrier semaphores. Data moves between devices by JAX's collectives and lax.ppermute only.
A program may use at most 128 MiB of HBM per device.

v0:
```python
import math
import jax
import jax.numpy as jnp
from jax import lax
from jax.sharding import PartitionSpec as P


def whiten(spectra):
    values = spectra.astype(jnp.float32)
    windows = values.shape[-1] // 2
    power_sum = values[..., :windows] ** 2 + values[..., windows:] ** 2
    amplitude = jnp.sqrt(jnp.mean(power_sum, axis=1, keepdims=True) + 1e-06)
    divisor = jnp.concatenate([amplitude, amplitude], -1)
    return (values / divisor).astype(jnp.bfloat16)


def lag_table(bin_count, lag_count):
    freq_index = jnp.arange(bin_count, dtype=jnp.int32)
    lag_index = jnp.arange(lag_count, dtype=jnp.int32)
    product = freq_index[:, None] * lag_index[None, :] % lag_count
    phase = product.astype(jnp.float32) * (2.0 * math.pi / lag_count)
    weight = 1.0 / math.sqrt(bin_count)
    return (jnp.stack([jnp.cos(phase), -jnp.sin(phase)]) * weight).astype(jnp.bfloat16)


def round_partners(group_count):
    last_label = group_count - 1
    round_label = jnp.arange(last_label, dtype=jnp.int32)[:, None]
    label_index = jnp.arange(group_count, dtype=jnp.int32)[None, :]
    opposite = jnp.mod(2 * round_label - label_index, last_label)
    inner = jnp.where(opposite == label_index, last_label, opposite)
    return jnp.where(label_index == last_label, round_label, inner)


def with_rotation(partner_blocks, windows, axis_at):
    rotated = jnp.concatenate([-partner_blocks[..., windows:], partner_blocks[..., :windows]], -1)
    return jnp.stack([partner_blocks, rotated], axis_at)


def shards(spectra):
    white = whiten(spectra)
    block_rows, bin_count, width_total = white.shape
    windows = width_total // 2
    norm_scale = 1.0 / math.sqrt(windows)
    lag_count = 2 * bin_count
    table = lag_table(bin_count, lag_count)
    pairing = round_partners(lax.axis_size("grp"))
    group_index = lax.axis_index("grp")
    partners = jnp.take(pairing, group_index, axis=1)
    collected = lax.all_gather(white, "grp", axis=0, tiled=True)
    collected = collected.reshape(-1, block_rows, bin_count, width_total)
    partner_blocks = jnp.take(collected, partners, axis=0)
    stacked = with_rotation(partner_blocks, windows, 1)
    flat_table = table.reshape(2 * bin_count, lag_count)
    spectrum = (
        jnp.einsum(
            "nfw,rsdfw->rndsf",
            lax.all_gather(white, "mem", axis=0, tiled=True),
            stacked,
            preferred_element_type=jnp.float32,
        )
        * norm_scale
    )
    spectrum = spectrum.astype(jnp.bfloat16)
    spectrum = spectrum.reshape(
        spectrum.shape[0], spectrum.shape[1], spectrum.shape[2], 2 * bin_count
    )
    correlated = jnp.einsum(
        "rndx,xl->rndl", spectrum, flat_table, preferred_element_type=jnp.float32
    ).astype(jnp.bfloat16)
    return correlated.reshape(
        correlated.shape[0], 1, correlated.shape[1], 1, correlated.shape[2], correlated.shape[3]
    )


def solution(mesh):
    return jax.shard_map(
        shards,
        mesh=mesh,
        in_specs=(P(("grp", "mem"), None, None),),
        out_specs=P(None, "grp", None, "mem", None, None),
        check_vma=False,
    )
```

profile of v0, /device:TPU:1, one launch (start us, length us, event | category | flops | bytes accessed | tf_op | source)
XLA Modules:
  0.0 558.8 jit_solution(15928825194021076410)
XLA Ops:
  6.5 0.0 all-gather.3.cloned.1.call-start
  6.5 1.2 convert_element_type.34
  7.7 0.3 fusion.12
  8.0 0.1 maximum_bitcast_fusion.1
  8.1 2.0 divide_convert_fusion
  10.1 0.0 all-gather.3.cloned.1.call-update
  10.1 0.0 all-gather.5.cloned.1.call-start
  10.2 0.7 all-gather.5.cloned.1.call-update
  10.9 0.1 fusion.27
  11.0 0.1 sine_negate_fusion
  11.2 59.0 %all-gather.3.cloned.1.call-done = bf16[96,64,384]{2,1,0:T(8,128)(2,1)} async-done(((bf16[12,64,384]{2,1,0:T(8,128)(2,1)}), bf16[96,64,384]{2,1,0:T(8,128)(2,1)}) %all-gather.3.cloned.1.call-update) | async-done | bytes 4718608 | tf_op jit(solution)/shard_map/all_gather | solution.py:50
  70.2 5.6 %gather_fusion = bf16[7,12,64,384]{3,2,1,0:T(8,128)(2,1)} fusion(bf16[8,12,64,384]{3,2,1,0:T(8,128)(2,1)} %bitcast.34, s32[1024]{0:T(1024)S(1)} %pad_clamp_fusion), kind=kCustom, calls=%fused_computation | custom fusion | bytes 8257564 | tf_op jit(solution)/shard_map/jit(_take)/gather | solution.py:52
  75.8 2.7 broadcast_select_fusion
  78.5 1.0 slice_negate_fusion
  79.5 0.0 copy-start
  79.5 1.6 maximum_bitcast_fusion
  81.2 0.5 copy-done
  81.7 2.4 bitcast_select_fusion
  84.1 6.4 %pad_maximum_fusion = bf16[7,2,12,64,384]{4,3,2,0,1:T(8,128)(2,1)} fusion(bf16[7,1,12,64,384]{4,3,2,0,1:T(8,128)(2,1)S(1)} %maximum_bitcast_fusion, bf16[7,1,12,64,384]{4,3,2,0,1:T(8,128)(2,1)} %bitcast_select_fusion), kind=kLoop, calls=%fused_computation.10 | loop fusion | flops 4128768 | bytes 16515072 | tf_op jit(solution)/shard_map/stack | solution.py:37
  90.5 389.9 %all-gather.5.cloned.1.call-done = bf16[384,64,384]{2,1,0:T(8,128)(2,1)} async-done(((bf16[12,64,384]{2,1,0:T(8,128)(2,1)}), bf16[384,64,384]{2,1,0:T(8,128)(2,1)}) %all-gather.5.cloned.1.call-update) | async-done | bytes 18874384 | tf_op jit(solution)/shard_map/all_gather | solution.py:58
  480.5 51.0 %fusion = f32[64,7,2,12,384]{4,3,2,1,0:T(8,128)} fusion(bf16[384,64,384,1,1]{2,1,0,3,4:T(8,128)(2,1)} %bitcast.33, bf16[7,2,12,64,384]{4,3,2,0,1:T(8,128)(2,1)} %pad_maximum_fusion), kind=kOutput, calls=%fused_computation.1 | convolution fusion | flops 3170893824 | bytes 43646976 | tf_op jit(solution)/shard_map/nfw,rsdfw->rndsf/dot_general | solution.py:56
  531.5 20.5 %fusion.7 = bf16[7,1,384,1,12,128]{5,2,4,3,1,0:T(8,128)(2,1)} fusion(f32[64,7,2,12,384]{4,3,2,1,0:T(8,128)} %fusion, f32[1,64,128]{2,1,0:T(8,128)S(1)} %get-tuple-element.18, f32[1,64,128]{2,1,0:T(8,128)S(1)} %get-tuple-element.19), kind=kOutput, calls=%fused_computation.9 | convolution fusion | flops 1069400064 | bytes 24838144 | tf_op jit(solution)/shard_map/rndx,xl->rndl/dot_general | solution.py:68
  (6 shorter events, 0.1 us)
Async XLA Ops:
  6.5 63.7 %all-gather.3.cloned.1.call-start = ((), (), s32[]{:S(2)}) async-start(), calls=%async_computation | async-start | bytes 5308416 | tf_op jit(solution)/shard_map/all_gather | solution.py:50
  10.1 470.3 %all-gather.5.cloned.1.call-start = ((), (), s32[]{:S(2)}) async-start(), calls=%async_computation.1 | async-start | bytes 19464192 | tf_op jit(solution)/shard_map/all_gather | solution.py:58
  79.5 2.2 copy-start
Sparse Core Ops, SparseCore 0:
  10.2 59.9 all-gather.2
  72.0 408.4 all-gather.4
where the time goes:
time: 559 us
  waiting for transfers between devices  450 us (81%)
  matrix products  71.5 us (13%)
  other arithmetic  18 us (3%)
  between operations  13.5 us (2%)
  local copies, waits for them, and re-layouts  6.11 us (1%)
    all_gather x1, waiting for transfers between devices, shards(): lax.all_gather(white, 'mem', axis=0, tiled=True)  390 us
    all_gather x1, waiting for transfers between devices, shards(): collected = lax.all_gather(white, 'grp', axis=0, tiled=True)  59 us
    dot_general x1, matrix products, shards(): jnp.einsum('nfw,rsdfw->rndsf', lax.all_gather(white, 'mem', axis=0, tiled...  51 us
    dot_general x1, matrix products, shards(): jnp.einsum('rndx,xl->rndl', spectrum, flat_table, preferred_element_type=...  20.5 us
  transfers between devices with their start and end apart: 2, of which 2 were waited for; matrix products, arithmetic and copies ran while one was open for 4% of the time, Pallas kernels for 0%

commit v1 on v0

--- a/solution.py
+++ b/solution.py
@@ -3,6 +3,11 @@
 import jax.numpy as jnp
 from jax import lax
 from jax.sharding import PartitionSpec as P
+
+
+def exchange_gather(shard, axis, dim):
+    sent = jnp.stack([shard] * lax.axis_size(axis))
+    return jnp.concatenate(lax.all_to_all(sent, axis, 0, 0), axis=dim)
 
 
 def whiten(spectra):
@@ -55,7 +60,7 @@
     spectrum = (
         jnp.einsum(
             "nfw,rsdfw->rndsf",
-            lax.all_gather(white, "mem", axis=0, tiled=True),
+            exchange_gather(white, "mem", 0),
             stacked,
             preferred_element_type=jnp.float32,
         )

time: 559 us -> 436 us (0.78)
  the two profiles are of different devices: /device:TPU:1 before, /device:TPU:238 now
where the time goes in v1:
time: 436 us; the launch traced here: 435 us
  waiting for transfers between devices  311 us (71%)
  matrix products  71.4 us (16%)
  other arithmetic  17.2 us (4%)
  between operations  13.5 us (3%)
  local copies, waits for them, and re-layouts  13.4 us (3%)
  starting transfers between devices  8.44 us (2%)
    all_to_all x1, waiting for transfers between devices, exchange_gather(): return jnp.concatenate(lax.all_to_all(sent, axis, 0, 0), axis=dim)  236 us
    all_gather x1, waiting for transfers between devices, shards(): collected = lax.all_gather(white, 'grp', axis=0, tiled=True)  74.7 us
    dot_general x1, matrix products, shards(): jnp.einsum('nfw,rsdfw->rndsf', exchange_gather(white, 'mem', 0), stacked,...  50.9 us
    dot_general x1, matrix products, shards(): jnp.einsum('rndx,xl->rndl', spectrum, flat_table, preferred_element_type=...  20.5 us
  transfers between devices with their start and end apart: 2, of which 2 were waited for; matrix products, arithmetic and copies ran while one was open for 5% of the time, Pallas kernels for 0%

profile of v1, /device:TPU:238, one launch (start us, length us, event | category | flops | bytes accessed | tf_op | source)
XLA Modules:
  0.0 435.1 jit_solution(5667507665595060588)
XLA Ops:
  6.5 1.2 convert_element_type.34
  7.7 0.3 fusion.12
  8.0 0.1 maximum_bitcast_fusion.1
  8.1 1.2 divide_convert_fusion
  9.3 0.0 copy-start.1
  9.3 7.2 %stack.10 = bf16[32,12,64,384]{3,2,1,0:T(8,128)(2,1)} broadcast(bf16[12,64,384]{2,1,0:T(8,128)(2,1)S(1)} %divide_convert_fusion), dimensions={1,2,3} | broadcast | bytes 19464192 | tf_op jit(solution)/shard_map/stack | solution.py:9
  16.5 0.0 copy-done.1
  16.5 8.4 %all-to-all-start = ((bf16[32,12,64,384]{3,2,1,0:T(8,128)(2,1)}), bf16[32,12,64,384]{3,2,1,0:T(8,128)(2,1)}, u32[]{:S(2)}, u32[]{:S(2)}) async-start(bf16[32,12,64,384]{3,2,1,0:T(8,128)(2,1)} %stack.10), calls=%async_computation | async-start | bytes 37748736 | tf_op jit(solution)/shard_map/all_to_all | solution.py:10
  24.9 0.0 all-gather.2.cloned.1.call-start
  25.0 0.7 all-gather.2.cloned.1.call-update
  25.7 0.1 fusion.27
  25.8 0.1 sine_negate_fusion
  26.0 74.7 %all-gather.2.cloned.1.call-done = bf16[96,64,384]{2,1,0:T(8,128)(2,1)} async-done(((bf16[12,64,384]{2,1,0:T(8,128)(2,1)}), bf16[96,64,384]{2,1,0:T(8,128)(2,1)}) %all-gather.2.cloned.1.call-update) | async-done | bytes 4718608 | tf_op jit(solution)/shard_map/all_gather | solution.py:55
  100.6 5.6 %gather_fusion = bf16[7,12,64,384]{3,2,1,0:T(8,128)(2,1)} fusion(bf16[8,12,64,384]{3,2,1,0:T(8,128)(2,1)} %bitcast.35, s32[1024]{0:T(1024)S(1)} %pad_clamp_fusion), kind=kCustom, calls=%fused_computation | custom fusion | bytes 8257564 | tf_op jit(solution)/shard_map/jit(_take)/gather | solution.py:57
  106.2 2.7 broadcast_select_fusion
  108.9 1.0 slice_negate_fusion
  109.9 0.0 copy-start
  109.9 1.6 maximum_bitcast_fusion
  111.6 0.5 copy-done
  112.1 2.5 bitcast_select_fusion
  114.5 6.4 %pad_maximum_fusion = bf16[7,2,12,64,384]{4,3,2,0,1:T(8,128)(2,1)} fusion(bf16[7,1,12,64,384]{4,3,2,0,1:T(8,128)(2,1)S(1)} %maximum_bitcast_fusion, bf16[7,1,12,64,384]{4,3,2,0,1:T(8,128)(2,1)} %bitcast_select_fusion), kind=kLoop, calls=%fused_computation.10 | loop fusion | flops 4128768 | bytes 16515072 | tf_op jit(solution)/shard_map/stack | solution.py:42
  121.0 235.9 %all-to-all-done = bf16[32,12,64,384]{3,2,1,0:T(8,128)(2,1)} async-done(((bf16[32,12,64,384]{3,2,1,0:T(8,128)(2,1)}), bf16[32,12,64,384]{3,2,1,0:T(8,128)(2,1)}, u32[]{:S(2)}, u32[]{:S(2)}) %all-to-all-start) | async-done | bytes 18874400 | tf_op jit(solution)/shard_map/all_to_all | solution.py:10
  356.9 50.9 %fusion = f32[64,7,2,12,384]{4,3,2,1,0:T(8,128)} fusion(bf16[384,64,384,1,1]{2,1,0,3,4:T(8,128)(2,1)} %bitcast.8, bf16[7,2,12,64,384]{4,3,2,0,1:T(8,128)(2,1)} %pad_maximum_fusion), kind=kOutput, calls=%fused_computation.1 | convolution fusion | flops 3170893824 | bytes 43646976 | tf_op jit(solution)/shard_map/nfw,rsdfw->rndsf/dot_general | solution.py:61
  407.8 20.5 %fusion.7 = bf16[7,1,384,1,12,128]{5,2,4,3,1,0:T(8,128)(2,1)} fusion(f32[64,7,2,12,384]{4,3,2,1,0:T(8,128)} %fusion, f32[1,64,128]{2,1,0:T(8,128)S(1)} %get-tuple-element.18, f32[1,64,128]{2,1,0:T(8,128)S(1)} %get-tuple-element.19), kind=kOutput, calls=%fused_computation.9 | convolution fusion | flops 1069400064 | bytes 24838144 | tf_op jit(solution)/shard_map/rndx,xl->rndl/dot_general | solution.py:73
  (6 shorter events, 0.1 us)
Async XLA Ops:
  9.3 7.2 %copy-start.1 = (bf16[12,64,384]{2,1,0:T(8,128)(2,1)}, bf16[12,64,384]{2,1,0:T(8,128)(2,1)S(1)}, u32[]{:S(2)}) copy-start(bf16[12,64,384]{2,1,0:T(8,128)(2,1)S(1)} %divide_convert_fusion) | copy-start | bytes 1769476
  16.5 340.4 %all-to-all-start = ((bf16[32,12,64,384]{3,2,1,0:T(8,128)(2,1)}), bf16[32,12,64,384]{3,2,1,0:T(8,128)(2,1)}, u32[]{:S(2)}, u32[]{:S(2)}) async-start(bf16[32,12,64,384]{3,2,1,0:T(8,128)(2,1)} %stack.10), calls=%async_computation | async-start | bytes 37748736 | tf_op jit(solution)/shard_map/all_to_all | solution.py:10
  24.9 75.7 %all-gather.2.cloned.1.call-start = ((), (), s32[]{:S(2)}) async-start(), calls=%async_computation.1 | async-start | bytes 5308416 | tf_op jit(solution)/shard_map/all_gather | solution.py:55
  109.9 2.2 copy-start
Sparse Core Ops, SparseCore 0:
  27.6 73.0 all-gather.1
